TPU v7x, 32 devices: a whole 2x2x4 slice. The times are simulated.
32 devices in a mesh: order: 4 (over z), band: 4 (over x, core), chan: 2 (over y).
Axes of the slice: x: 2, y: 2, z: 4, core: 2. Of those that a mesh axis runs over, the one named last changes fastest.
Arguments:
- coef_grad: bfloat16 [2, 368, 2, 384, 361], P('chan', ('order', 'band')), may hold values from -6 to 6
- coef_saved: bfloat16 [2, 368, 2, 73, 361], P('chan', ('order', 'band')), may hold values from -0.016601562 to 0.016601562
- lift_weight: bfloat16 [384, 73], replicated, may hold values from -0.3125 to 0.3125
- legendre: bfloat16 [368, 361, 16], P(('order', 'band')), may hold values from -0.3125 to 0.3125
- order_of_slot: int32 [368], replicated, may hold values from 0 to 367, as said below
- trunc_degree: int32 [2], P('chan'), may hold values from 271 to 360
Outputs:
- grid_grad: bfloat16 [2, 73, 16, 1440], P('chan', None, ('order', 'band'))
- weight_grad: float32 [384, 73], P(('order', 'band'))
Inputs may be any that keep to these rules, and one draw needn't show every extreme that they name: order_of_slot holds each of 0 to 367 once; in the g-th block of 23 slots, slot s holds s * 16 + k_g for even s and s * 16 + 15 - k_g for odd s, where k is a permutation of 0 to 15.
All inputs are finite; a program needn't handle non-finite values.
Results may differ from a plain program's by a relative error of at most 0.0062.
Values may be sent and summed in bfloat16 or wider, within the bound.
No kernel may reach another device: no remote copies, remote signals or barrier semaphores. Data moves between devices by JAX's collectives and lax.ppermute only.
A program may use at most 64 MiB of HBM per device.

v0:
```python
import math

import jax
import jax.numpy as jnp
from jax import lax
from jax.sharding import PartitionSpec as P

LON = 1440


def local(coef_grad, coef_saved, lift_weight, legendre, order_of_slot, trunc_degree):
    samp_dev = coef_grad.shape[0]
    slot_dev = coef_grad.shape[1]
    degrees = coef_grad.shape[4]
    chan_in = coef_saved.shape[3]
    pair_width = 2 * chan_in
    groups = lax.axis_size(("order", "band"))
    slot_count = order_of_slot.shape[0]
    first_slot = lax.axis_index(("order", "band")) * slot_dev
    local_orders = lax.dynamic_slice_in_dim(order_of_slot, first_slot, slot_dev)
    degree_ids = jnp.arange(degrees, dtype=jnp.int32)
    live_mask = (degree_ids[None, None, :] >= local_orders[None, :, None]) & (
        degree_ids[None, None, :] <= trunc_degree[:, None, None]
    )
    kept_grad = jnp.where(live_mask[:, :, None, None, :], coef_grad, jnp.zeros((), coef_grad.dtype))
    lifted = jnp.einsum(
        "pqrel,ec->pqrcl", kept_grad, lift_weight, preferred_element_type=jnp.float32
    ).astype(jnp.bfloat16)
    lifted = lifted.reshape(samp_dev, slot_dev, pair_width, degrees)
    own_rows = lax.psum_scatter(
        jnp.einsum("pqrel,pqrcl->ec", kept_grad, coef_saved, preferred_element_type=jnp.float32),
        ("order", "band"),
        scatter_dimension=0,
        tiled=True,
    )
    weight_grad = lax.psum(own_rows, "chan")
    spectral = jnp.einsum(
        "qlt,pqjl->pqtj", legendre, lifted, preferred_element_type=jnp.float32
    ).astype(jnp.bfloat16)
    lat_dev = spectral.shape[2] // groups
    lon_ids = jnp.arange(LON, dtype=jnp.int32)
    angles = (order_of_slot[:, None] * lon_ids[None, :] % LON).astype(jnp.float32) * (
        2.0 * math.pi / LON
    )
    angle_table = jnp.stack([jnp.cos(angles), -jnp.sin(angles)], axis=1).astype(jnp.bfloat16)
    synth_scale = 1.0 / math.sqrt(LON)
    received = lax.all_to_all(spectral, ("order", "band"), split_axis=2, concat_axis=1, tiled=True)
    item_count = received.shape[0]
    split_parts = received.reshape(item_count, slot_count, lat_dev, 2, chan_in)
    synth_field = jnp.einsum(
        "pqtrc,qrn->pctn", split_parts, angle_table, preferred_element_type=jnp.float32
    )
    grid_grad = (synth_field * synth_scale).astype(jnp.bfloat16)
    return (grid_grad, weight_grad)


def solution(mesh):
    return jax.shard_map(
        local,
        mesh=mesh,
        in_specs=(
            P("chan", ("order", "band"), None, None, None),
            P("chan", ("order", "band"), None, None, None),
            P(),
            P(("order", "band"), None, None),
            P(),
            P("chan"),
        ),
        out_specs=(P("chan", None, ("order", "band"), None), P(("order", "band"), None)),
        check_vma=False,
    )
```

profile of v0, /device:TPU:0, one launch (start us, length us, event | category | flops | bytes accessed | tf_op | source)
XLA Modules:
  0.0 113.4 jit_solution(15885522489254012622)
XLA Ops:
  7.2 0.0 copy-start
  7.2 0.0 reduce-scatter.4.cloned.1.call-start
  8.0 0.8 dynamic_slice.3
  8.8 0.1 fusion.34
  8.9 19.3 %fusion = bf16[23,2,384,361]{2,1,3,0:T(2,128)(2,1)S(1)} fusion(bf16[1,23,2,384,361]{3,2,4,1,0:T(2,128)(2,1)} %param.6, pred[23,361]{1,0:T(8,128)(4,1)S(1)} %fusion.34), kind=kLoop, calls=%fused_computation.1 | loop fusion | flops 6376704 | bytes 25515120 | tf_op jit(solution)/shard_map/reshape.9
  28.2 0.0 copy-done
  28.2 0.0 copy-start.1
  28.2 4.6 %copy-done.1 = bf16[23,2,384,361]{2,1,3,0:T(2,128)(2,1)} copy-done((bf16[23,2,384,361]{2,1,3,0:T(2,128)(2,1)}, bf16[23,2,384,361]{2,1,3,0:T(2,128)(2,1)S(1)}, u32[]{:S(2)}) %copy-start.1) | copy-done | bytes 12753432
  32.8 4.7 %fusion.24 = f32[384,73]{1,0:T(8,128)} fusion(bf16[23,2,73,361]{3,1,2,0:T(2,128)(2,1)S(1)} %bitcast.44, bf16[23,2,384,361]{2,1,3,0:T(2,128)(2,1)S(1)} %fusion), kind=kOutput, calls=%fused_computation.27 | convolution fusion | flops 930998784 | bytes 15290012 | tf_op jit(solution)/shard_map/pqrel,pqrcl->ec/dot_general | solution.py:31
  37.4 0.0 reduce-scatter.4.cloned.1.call-update
  37.5 0.0 copy-done.4
  37.5 9.0 %convert_bitcast_fusion = bf16[1,23,2,73,361]{4,3,2,1,0:T(8,128)(2,1)S(1)} fusion(bf16[23,2,384,361]{2,1,3,0:T(2,128)(2,1)} %copy-done.1, bf16[384,73]{0,1:T(8,128)(2,1)S(1)} %copy-done.4), kind=kOutput, calls=%fused_computation.8 | convolution fusion | flops 932211008 | bytes 15233948 | tf_op jit(solution)/shard_map/pqrel,ec->pqrcl/dot_general | solution.py:26
  46.5 1.0 copy.19
  47.5 0.0 copy-start.2
  47.6 0.0 copy-done.3
  47.6 1.0 fusion.29
  48.6 0.8 copy.21
  49.4 7.4 %all-to-all-start = ((bf16[1,23,16,146]{3,1,0,2:T(8,128)(2,1)}), bf16[1,23,16,146]{3,1,0,2:T(8,128)(2,1)S(1)}, u32[]{:S(2)}, u32[]{:S(2)}) async-start(bf16[1,23,16,146]{3,1,0,2:T(8,128)(2,1)} %copy.21), calls=%async_computation | async-start | bytes 393216 | tf_op jit(solution)/shard_map/all_to_all | solution.py:47
  56.7 10.4 %cosine_convert_fusion = (bf16[368,1,1440]{0,2,1:T(8,128)(2,1)}, bf16[368,1,1440]{0,2,1:T(8,128)(2,1)}) fusion(s32[368]{0:T(512)S(1)} %copy-done.2), kind=kLoop, calls=%fused_computation.21 | loop fusion | flops 6359040 | bytes 2121152 | tf_op jit(solution)/shard_map/convert
  67.2 26.8 %reduce-scatter.4.cloned.1.call-done = f32[24,73]{1,0:T(8,128)} async-done(((f32[384,73]{1,0:T(8,128)}), f32[24,73]{1,0:T(8,128)}) %reduce-scatter.4.cloned.1.call-update) | async-done | bytes 7024
  94.0 9.3 %psum.7 = f32[24,73]{1,0:T(8,128)} all-reduce(f32[24,73]{1,0:T(8,128)} %reduce-scatter.4.cloned.1.call-done), channel_id=1, replica_groups=mesh['order'=4,'band'=4,'chan'=2] {'chan'}, use_global_device_ids=true, to_apply=%region_1.2 | all-reduce | flops 1752 | bytes 14016 | tf_op jit(solution)/shard_map/psum | solution.py:36
  103.3 0.0 all-to-all-done
  103.3 0.2 reshape.167
  103.5 3.1 %fusion.10 = bf16[1,73,1,1440]{3,1,2,0:T(8,128)(2,1)} fusion(bf16[368,1,1440]{0,2,1:T(8,128)(2,1)} %get-tuple-element.3, bf16[368,1,1440]{0,2,1:T(8,128)(2,1)} %get-tuple-element.2, bf16[368,2,73]{2,1,0:T(2,128)(2,1)S(1)} %reshape.167), kind=kOutput, calls=%fused_computation.14 | convolution fusion | flops 156006720 | bytes 2437376 | tf_op jit(solution)/shard_map/pqtrc,qrn->pctn/dot_general | solution.py:50
  (4 shorter events, 0.0 us)
Async XLA Ops:
  7.2 21.0 %copy-start = (bf16[1,23,2,73,361]{4,2,3,1,0:T(2,128)(2,1)S(1)}, bf16[1,23,2,73,361]{4,2,3,1,0:T(2,128)(2,1)}, u32[]{:S(2)}) copy-start(bf16[1,23,2,73,361]{4,2,3,1,0:T(2,128)(2,1)} %param.7) | copy-start | bytes 7273432
  7.2 86.8 %reduce-scatter.4.cloned.1.call-start = ((), (), s32[]{:S(2)}) async-start(), calls=%async_computation.2 | async-start | bytes 208896
  28.2 4.6 %copy-start.1 = (bf16[23,2,384,361]{2,1,3,0:T(2,128)(2,1)}, bf16[23,2,384,361]{2,1,3,0:T(2,128)(2,1)S(1)}, u32[]{:S(2)}) copy-start(bf16[23,2,384,361]{2,1,3,0:T(2,128)(2,1)S(1)} %fusion) | copy-start | bytes 38260228
  32.8 4.7 %copy-start.4 = (bf16[384,73]{0,1:T(8,128)(2,1)S(1)}, bf16[384,73]{0,1:T(8,128)(2,1)}, u32[]{:S(2)}) copy-start(bf16[384,73]{0,1:T(8,128)(2,1)} %param.8) | copy-start | bytes 168196
  46.5 1.0 copy-start.3
  47.5 9.2 %copy-start.2 = (s32[368]{0:T(512)S(1)}, s32[368]{0:T(512)}, u32[]{:S(2)}) copy-start(s32[368]{0:T(512)} %param.10) | copy-start | bytes 4420
  49.4 54.0 %all-to-all-start = ((bf16[1,23,16,146]{3,1,0,2:T(8,128)(2,1)}), bf16[1,23,16,146]{3,1,0,2:T(8,128)(2,1)S(1)}, u32[]{:S(2)}, u32[]{:S(2)}) async-start(bf16[1,23,16,146]{3,1,0,2:T(8,128)(2,1)} %copy.21), calls=%async_computation | async-start | bytes 393216 | tf_op jit(solution)/shard_map/all_to_all | solution.py:47
Sparse Core Ops, SparseCore 0:
  37.6 56.3 reduce-scatter.3
where the time goes:
time: 114 us; the launch traced here: 113 us
  other arithmetic  29.8 us (26%)
  waiting for transfers between devices  26.8 us (24%)
  matrix products  17.8 us (16%)
  between operations  14.9 us (13%)
  blocking collectives  9.35 us (8%)
  starting transfers between devices  7.4 us (6%)
  local copies, waits for them, and re-layouts  7.26 us (6%)
    another operation x2, other arithmetic  29.7 us
    unnamed x2, waiting for transfers between devices  26.8 us
    psum x1, blocking collectives, local(): weight_grad = lax.psum(own_rows, 'chan')  9.35 us
    dot_general x1, matrix products, local(): jnp.einsum('pqrel,ec->pqrcl', kept_grad, lift_weight, preferred_element_t...  9.05 us
    all_to_all x1, starting transfers between devices, local(): lax.all_to_all(spectral, ('order', 'band'), split_axis=2, concat_axis=1,...  7.36 us
    dot_general x1, matrix products, local(): jnp.einsum('pqrel,pqrcl->ec', kept_grad, coef_saved, preferred_element_ty...  4.66 us
    unnamed x10, local copies, waits for them, and re-layouts  4.58 us
    dot_general x1, matrix products, local(): jnp.einsum('pqtrc,qrn->pctn', split_parts, angle_table, preferred_element...  3.07 us
  transfers between devices with their start and end apart: 2, of which 1 were waited for; matrix products, arithmetic and copies ran while one was open for 20% of the time, Pallas kernels for 0%

commit v1 on v0

v1 whole, which is shorter than its diff:
```python
import math

import jax
import jax.numpy as jnp
from jax import lax
from jax.experimental import pallas as pl
from jax.experimental.pallas import tpu as pltpu
from jax.sharding import PartitionSpec as P

LON = 1440
LANES = 128
GROUP_AXES = ("order", "band")


def round_up(value, step):
    return -(-value // step) * step


def slot_classes(slots, groups, degrees):
    classes = {}
    for slot in range(slots):
        low = groups * slot
        if low < degrees:
            classes.setdefault(low // LANES, []).append(slot)
    return [(tile, found[0], found[-1] + 1) for tile, found in sorted(classes.items())]


def lane_tiles(degrees):
    return [(at, min(LANES, degrees - at)) for at in range(0, degrees, LANES)]


def spectral_kernel(groups, pad_slots, order_hbm, trunc_hbm, grad_hbm, saved_hbm, legendre_hbm, weight_hbm,
                    out_ref, order_ref, trunc_ref, legendre_buf, weight_buf, grad_buf, *rest):
    slots, degrees, _, embed = grad_hbm.shape
    chan_in = weight_hbm.shape[0]
    chan_pad = round_up(chan_in, 8)
    lats = legendre_hbm.shape[1]
    tiles = lane_tiles(degrees)
    saved_bufs = rest[: len(tiles)]
    grad_wide, saved_wide, spec_wide, weight_acc, weight_turned, small_sem, grad_sem, saved_sem = rest[len(tiles):]
    small_copies = [
        pltpu.make_async_copy(source, target, small_sem.at[at])
        for at, (source, target) in enumerate([
            (order_hbm, order_ref), (trunc_hbm, trunc_ref), (legendre_hbm, legendre_buf), (weight_hbm, weight_buf)
        ])
    ]
    for copy in small_copies:
        copy.start()
    embed_tiles = embed // LANES
    classes = slot_classes(slots, groups, degrees)

    def grad_copies(slot, tile):
        rows = pl.ds(tile * LANES, degrees - tile * LANES)
        return [
            pltpu.make_async_copy(
                grad_hbm.at[slot, rows, :, pl.ds(at * LANES, LANES)],
                grad_buf.at[slot, at, rows],
                grad_sem.at[slot, at],
            )
            for at in range(embed_tiles)
        ]

    def saved_copies(slot, tile):
        return [
            pltpu.make_async_copy(
                saved_hbm.at[slot, :, :, pl.ds(*tiles[at])],
                saved_bufs[at].at[slot, pl.ds(0, chan_in)],
                saved_sem.at[slot, at],
            )
            for at in range(tile, len(tiles))
        ]

    for tile, first, last in classes:
        @pl.loop(first, last)
        def _(slot):
            for copy in grad_copies(slot, tile) + saved_copies(slot, tile):
                copy.start()

    spec_wide[...] = jnp.zeros_like(spec_wide)
    weight_acc[...] = jnp.zeros_like(weight_acc)
    for at in range(embed_tiles):
        grad_wide[at, 2 * degrees // 8 * 8 :] = jnp.zeros((grad_wide.shape[1] - 2 * degrees // 8 * 8, LANES), jnp.float32)
    for copy in small_copies:
        copy.wait()
    first_slot = (lax.axis_index("order") * lax.axis_size("band") + lax.axis_index("band")) * slots
    top = trunc_ref[0]
    for tile, first, last in classes:
        low = tile * LANES
        live = degrees - low
        live_pad = round_up(live, LANES)

        @pl.loop(first, last)
        def _(slot):
            for copy in grad_copies(slot, tile) + saved_copies(slot, tile):
                copy.wait()
            order = order_ref[first_slot + slot]
            degree = lax.broadcasted_iota(jnp.int32, (1, live_pad), 1) + low
            mask = (degree >= order) & (degree <= top)
            for at in range(embed_tiles):
                pairs = grad_buf[slot, at, low:degrees].reshape(2 * live, LANES)
                grad_wide[at, : 2 * live] = pairs.astype(jnp.float32)
            for at in range(tile, len(tiles)):
                start, width = tiles[at]
                pairs = saved_bufs[at][slot, :chan_in].reshape(2 * chan_in, width)
                saved_wide[at, : 2 * chan_in, :width] = pairs.astype(jnp.float32)
            lat_rows = legendre_buf[slot, :, low:degrees]
            lat_rows = jnp.where(mask[:, :live], lat_rows.astype(jnp.float32), 0.0).astype(jnp.bfloat16)
            for part in range(2):
                grads = jnp.concatenate(
                    [grad_wide[at, pl.ds(part, live_pad, stride=2)].astype(jnp.bfloat16) for at in range(embed_tiles)],
                    axis=1,
                )
                saved = jnp.concatenate(
                    [saved_wide[at, pl.ds(part, chan_pad, stride=2)] for at in range(tile, len(tiles))], axis=1
                )
                saved = jnp.where(mask, saved, 0.0).astype(jnp.bfloat16)
                lifted = lax.dot_general(
                    grads, weight_buf[...], (((1,), (1,)), ((), ())), preferred_element_type=jnp.float32
                ).astype(jnp.bfloat16)
                spec = jnp.dot(lat_rows, lifted[:live], preferred_element_type=jnp.float32)
                row = pl.multiple_of((part * pad_slots + slot) * lats, lats)
                spec_wide[pl.ds(row, lats), :chan_in] = spec
                weight_acc[:chan_pad] += jnp.dot(saved, grads, preferred_element_type=jnp.float32)

    for at in range(embed_tiles):
        weight_turned[at * LANES : (at + 1) * LANES] = weight_acc[:, at * LANES : (at + 1) * LANES].T
    rows_dev = embed // groups
    head = LANES - chan_in
    lane = lax.broadcasted_iota(jnp.int32, (2 * pad_slots, LANES), 1)
    for group in range(groups):
        block = weight_turned[group * rows_dev : (group + 1) * rows_dev]
        shifted = [pltpu.roll(block, chan_in, 1), pltpu.roll(block, chan_in - head, 1)]
        if rows_dev < pad_slots:
            fill = jnp.zeros((pad_slots - rows_dev, LANES), jnp.float32)
            shifted = [shifted[0], fill, shifted[1], fill]
        spec = spec_wide[pl.ds(group, 2 * pad_slots, stride=lats)]
        both = jnp.where(lane < chan_in, spec, jnp.concatenate(shifted, axis=0))
        out_ref[group] = both.astype(jnp.bfloat16)


def table_kernel(groups, slots, order_ref, table_ref):
    pad_slots = table_ref.shape[0] // (2 * groups)
    shape = (pad_slots, LANES)
    slot = lax.broadcasted_iota(jnp.int32, shape, 0)
    lane = lax.broadcasted_iota(jnp.int32, shape, 1)

    def circle(steps):
        steps = steps.astype(jnp.float32)
        turns = jnp.floor(steps * (1.0 / LON) + 0.5)
        half = (steps - turns * LON) * (math.pi / LON)
        square = half * half
        sine = 1.0
        for power in (11, 9, 7, 5, 3):
            sine = 1.0 - square * sine * (1.0 / (power * (power - 1)))
        sine = sine * half
        cosine = 1.0
        for power in (12, 10, 8, 6, 4, 2):
            cosine = 1.0 - square * cosine * (1.0 / (power * (power - 1)))
        return 1.0 - 2.0 * sine * sine, 2.0 * sine * cosine

    @pl.loop(0, groups)
    def _(group):
        key = order_ref[group * slots]
        order = slot * groups + jnp.where(slot % 2 == 0, key, groups - 1 - key)
        cosine, sine = circle(order * lane)
        turn_cosine, turn_sine = circle(order * LANES)
        row = pl.multiple_of(group * 2 * pad_slots, 2 * pad_slots)
        for at in range(0, LON, LANES):
            width = min(LANES, LON - at)
            both = jnp.concatenate([cosine, -sine], axis=0).astype(jnp.bfloat16)
            table_ref[pl.ds(row, 2 * pad_slots), at : at + width] = both[:, :width]
            cosine, sine = (
                cosine * turn_cosine - sine * turn_sine,
                sine * turn_cosine + cosine * turn_sine,
            )


def weight_kernel(chan_in, rows_dev, items_ref, sum_ref):
    groups, rows, _ = items_ref.shape
    pad_slots = rows // 2
    total = items_ref[0].astype(jnp.float32)
    for group in range(1, groups):
        total = total + items_ref[group].astype(jnp.float32)
    head = LANES - chan_in
    lane = lax.broadcasted_iota(jnp.int32, (pad_slots, LANES), 1)
    near = pltpu.roll(total[:pad_slots], LANES - chan_in, 1)
    far = pltpu.roll(total[pad_slots:], LANES - (chan_in - head), 1)
    sum_ref[...] = jnp.where(lane < head, near, far)[:rows_dev, :chan_in]


def synthesis_kernel(items_ref, table_ref, field_ref):
    chan_in = field_ref.shape[0]
    groups, rows, _ = items_ref.shape
    items = items_ref[...].reshape(groups * rows, LANES)
    field = lax.dot_general(
        items, table_ref[...], (((0,), (0,)), ((), ())), preferred_element_type=jnp.float32
    )
    field_ref[...] = (field[:chan_in] * (1.0 / math.sqrt(LON))).astype(jnp.bfloat16)


def local(coef_grad, coef_saved, lift_weight, legendre, order_of_slot, trunc_degree):
    _, slots, _, embed, degrees = coef_grad.shape
    chan_in = coef_saved.shape[3]
    lats = legendre.shape[2]
    groups = lax.axis_size(GROUP_AXES)
    samples = lax.axis_size("chan")
    rows_dev = embed // groups
    pad_slots = max(round_up(slots, 8), round_up(rows_dev, 8))
    rows = 2 * pad_slots
    embed_tiles = embed // LANES
    tiles = lane_tiles(degrees)
    assert coef_grad.shape[0] == 1 and lats == groups and 2 * (LANES - chan_in) >= chan_in

    smem = pl.BlockSpec(memory_space=pltpu.SMEM)
    vmem = pl.BlockSpec(memory_space=pltpu.VMEM)
    hbm = pl.BlockSpec(memory_space=pltpu.HBM)
    grad_view = jnp.transpose(coef_grad[0], (0, 3, 1, 2))
    saved_view = jnp.transpose(coef_saved[0], (0, 2, 1, 3))
    packed = pl.pallas_call(
        lambda *refs: spectral_kernel(groups, pad_slots, *refs),
        out_shape=jax.ShapeDtypeStruct((groups, rows, LANES), jnp.bfloat16),
        in_specs=[hbm] * 6,
        out_specs=vmem,
        scratch_shapes=[
            pltpu.SMEM(order_of_slot.shape, jnp.int32),
            pltpu.SMEM(trunc_degree.shape, jnp.int32),
            pltpu.VMEM((slots, lats, degrees), jnp.bfloat16),
            pltpu.VMEM((chan_in, embed), jnp.bfloat16),
            pltpu.VMEM((slots, embed_tiles, round_up(degrees, 8), 2, LANES), jnp.bfloat16),
            *[pltpu.VMEM((slots, round_up(chan_in, 8), 2, width), jnp.bfloat16) for _, width in tiles],
            pltpu.VMEM((embed_tiles, 2 * round_up(degrees, LANES) + 8, LANES), jnp.float32),
            pltpu.VMEM((len(tiles), 2 * round_up(chan_in, 8) + 8, LANES), jnp.float32),
            pltpu.VMEM(((rows + 1) * lats, LANES), jnp.float32),
            pltpu.VMEM((LANES, embed), jnp.float32),
            pltpu.VMEM((embed, LANES), jnp.float32),
            pltpu.SemaphoreType.DMA((4,)),
            pltpu.SemaphoreType.DMA((slots, embed_tiles)),
            pltpu.SemaphoreType.DMA((slots, len(tiles))),
        ],
        compiler_params=pltpu.CompilerParams(vmem_limit_bytes=60 << 20),
        name="spectral",
    )(order_of_slot, trunc_degree, grad_view, saved_view, jnp.transpose(legendre, (0, 2, 1)), lift_weight.T)

    received = lax.all_to_all(packed, GROUP_AXES, split_axis=0, concat_axis=0, tiled=True)

    table = pl.pallas_call(
        lambda *refs: table_kernel(groups, slots, *refs),
        out_shape=jax.ShapeDtypeStruct((groups * rows, LON), jnp.bfloat16),
        in_specs=[smem],
        out_specs=vmem,
        cost_estimate=pl.CostEstimate(flops=20_000_000, bytes_accessed=groups * rows * LON * 2, transcendentals=0),
        name="table",
    )(order_of_slot)

    own = pl.pallas_call(
        lambda *refs: weight_kernel(chan_in, rows_dev, *refs),
        out_shape=jax.ShapeDtypeStruct((rows_dev, chan_in), jnp.float32),
        in_specs=[vmem],
        out_specs=vmem,
        name="weight_rows",
    )(received)
    if samples == 2:
        weight_grad = own + lax.ppermute(own, "chan", [(0, 1), (1, 0)])
    else:
        weight_grad = lax.psum(own, "chan")

    field = pl.pallas_call(
        synthesis_kernel,
        out_shape=jax.ShapeDtypeStruct((chan_in, LON), jnp.bfloat16),
        in_specs=[vmem, vmem],
        out_specs=vmem,
        cost_estimate=pl.CostEstimate(flops=2 * groups * rows * LANES * LON, bytes_accessed=groups * rows * LON * 2, transcendentals=0),
        name="synthesis",
    )(received, table)
    return (field[None, :, None, :], weight_grad)


def solution(mesh):
    return jax.shard_map(
        local,
        mesh=mesh,
        in_specs=(
            P("chan", GROUP_AXES, None, None, None),
            P("chan", GROUP_AXES, None, None, None),
            P(),
            P(GROUP_AXES, None, None),
            P(),
            P("chan"),
        ),
        out_specs=(P("chan", None, GROUP_AXES, None), P(GROUP_AXES, None)),
        check_vma=False,
    )
```

time: 114 us -> 48 us (0.42)
  Pallas kernels: 0 us -> 30.8 us
  other arithmetic: 29.8 us -> 0.6 us
  waiting for transfers between devices: 26.8 us -> 5.42 us
  matrix products: 17.8 us -> 0 us
  between operations: 14.9 us -> 1.3 us
  blocking collectives: 9.35 us -> 0 us
  local copies, waits for them, and re-layouts: 7.26 us -> 0.69 us
  starting transfers between devices: 7.4 us -> 8.89 us
    pallas_call x0 -> x4, Pallas kernels: none -> 30.8 us  [the longest x1 22.6 us: local(): pl.pallas_call(lambda *refs: spectral_kernel(groups, pad_slots, *refs), o...]
    another operation x2 -> x0, other arithmetic: 29.7 us -> none
    unnamed x2 -> x0, waiting for transfers between devices: 26.8 us -> none
    dot_general x4 -> x0, matrix products: 17.8 us -> none  [the longest x1 9.05 us: local(): jnp.einsum('pqrel,ec->pqrcl', kept_grad, lift_weight, preferred_element_t...]
    psum x1 -> x0, blocking collectives: 9.35 us -> none  [local(): weight_grad = lax.psum(own_rows, 'chan')]
    all_to_all x1, waiting for transfers between devices: 0.01 us -> 5.42 us  [local(): lax.all_to_all(packed, GROUP_AXES, split_axis=0, concat_axis=0, tiled=True)]
    unnamed x10 -> x4, local copies, waits for them, and re-layouts: 4.58 us -> 0.69 us
    convert_element_type x2 -> x0, local copies, waits for them, and re-layouts: 1.76 us -> none  [the longest x1 1 us: local(): lifted = jnp.einsum('pqrel,ec->pqrcl', kept_grad, lift_weight, preferred_...]
  transfers between devices with their start and end apart: 2 -> 2, of which waited for: 1 -> 1; matrix products, arithmetic and copies ran while one was open for 20% -> 0% of each run, Pallas kernels for 0% -> 14%
where the time goes in v1:
time: 48 us; the launch traced here: 47.7 us
  Pallas kernels  30.8 us (64%)
  starting transfers between devices  8.89 us (19%)
  waiting for transfers between devices  5.42 us (11%)
  between operations  1.3 us (3%)
  local copies, waits for them, and re-layouts  0.69 us (1%)
  other arithmetic  0.6 us (1%)
    pallas_call x1, Pallas kernels, local(): pl.pallas_call(lambda *refs: spectral_kernel(groups, pad_slots, *refs), o...  22.6 us
    all_to_all x1, starting transfers between devices, local(): lax.all_to_all(packed, GROUP_AXES, split_axis=0, concat_axis=0, tiled=True)  7.37 us
    all_to_all x1, waiting for transfers between devices, local(): lax.all_to_all(packed, GROUP_AXES, split_axis=0, concat_axis=0, tiled=True)  5.42 us
    pallas_call x1, Pallas kernels, local(): pl.pallas_call(lambda *refs: table_kernel(groups, slots, *refs), out_shap...  3.58 us
    pallas_call x1, Pallas kernels, local(): pl.pallas_call(synthesis_kernel, out_shape=jax.ShapeDtypeStruct((chan_in,...  2.97 us
    pallas_call x1, Pallas kernels, local(): pl.pallas_call(lambda *refs: weight_kernel(chan_in, rows_dev, *refs), out...  1.62 us
    ppermute x1, starting transfers between devices, local(): weight_grad = own + lax.ppermute(own, 'chan', [(0, 1), (1, 0)])  1.52 us
  transfers between devices with their start and end apart: 2, of which 1 were waited for; matrix products, arithmetic and copies ran while one was open for 0% of the time, Pallas kernels for 14%

profile of v1, /device:TPU:0, one launch (start us, length us, event | category | flops | bytes accessed | tf_op | source)
XLA Modules:
  0.0 47.7 jit_solution(9594096872518132165)
XLA Ops:
  1.3 22.6 %spectral.1 = bf16[16,48,128]{2,1,0:T(8,128)(2,1)} custom-call(s32[368]{0:T(512)} %refs_0_.3, s32[1]{0:T(128)S(6)} %copy.8.refs_1_, bf16[23,361,2,384]{3,2,1,0:T(2,128)(2,1)} %bitcast.9, bf16[23,73,2,361]{3,2,1,0:T(2,128)(2,1)} %bitcast.10, bf16[23,16,361]{2,1,0:T(8,128)(2,1)} %bitcast.11, bf16[73,384]{1,0:T(8,128)(2,1)} %bitcast.13), custom_call_target="tpu_custom_call" | custom-call | tf_op jit(solution)/shard_map/spectral/pallas_call | solution.py:219
  23.9 7.4 %all-to-all-start = ((bf16[16,48,128]{2,1,0:T(8,128)(2,1)}), bf16[16,48,128]{2,1,0:T(8,128)(2,1)S(1)}, u32[]{:S(2)}, u32[]{:S(2)}) async-start(bf16[16,48,128]{2,1,0:T(8,128)(2,1)} %spectral.1), calls=%async_computation | async-start | bytes 393216 | tf_op jit(solution)/shard_map/all_to_all | solution.py:244
  31.3 3.6 %table.1.table_ref = bf16[768,1440]{1,0:T(8,128)(2,1)} custom-call(s32[368]{0:T(512)} %refs_0_.3), custom_call_target="tpu_custom_call" | custom-call | flops 20000000 | bytes 2211840 | tf_op jit(solution)/shard_map/table/pallas_call | solution.py:246
  34.9 5.4 %all-to-all-done.items_ref.refs_0_ = bf16[16,48,128]{2,1,0:T(8,128)(2,1)S(1)} async-done(((bf16[16,48,128]{2,1,0:T(8,128)(2,1)}), bf16[16,48,128]{2,1,0:T(8,128)(2,1)S(1)}, u32[]{:S(2)}, u32[]{:S(2)}) %all-to-all-start) | async-done | bytes 196640 | tf_op jit(solution)/shard_map/all_to_all | solution.py:244
  40.3 0.0 copy-start
  40.3 0.7 %copy-done = bf16[16,48,128]{2,1,0:T(8,128)(2,1)} copy-done((bf16[16,48,128]{2,1,0:T(8,128)(2,1)}, bf16[16,48,128]{2,1,0:T(8,128)(2,1)S(1)}, u32[]{:S(2)}) %copy-start) | copy-done | bytes 196632
  41.0 1.6 %weight_rows.1 = f32[24,73]{1,0:T(8,128)} custom-call(bf16[16,48,128]{2,1,0:T(8,128)(2,1)} %copy-done), custom_call_target="tpu_custom_call" | custom-call | tf_op jit(solution)/shard_map/weight_rows/pallas_call | solution.py:255
  42.6 0.0 copy-start.1
  42.6 1.5 %collective-permute-start = (f32[24,73]{1,0:T(8,128)}, f32[24,73]{1,0:T(8,128)S(1)}, u32[]{:S(2)}, u32[]{:S(2)}) collective-permute-start(f32[24,73]{1,0:T(8,128)} %weight_rows.1), channel_id=1, source_target_pairs={{0,1},{1,0},{2,3},{3,2},{4,5},{5,4},{6,7},{7,6},{8,9},{9,8},{10,11... | collective-permute-start | bytes 21032 | tf_op jit(solution)/shard_map/ppermute | solution.py:263
  44.1 3.0 %synthesis.1 = bf16[73,1440]{1,0:T(8,128)(2,1)} custom-call(bf16[16,48,128]{2,1,0:T(8,128)(2,1)} %copy-done, bf16[768,1440]{1,0:T(8,128)(2,1)} %table.1.table_ref), custom_call_target="tpu_custom_call" | custom-call | flops 283115520 | bytes 2211840 | tf_op jit(solution)/shard_map/synthesis/pallas_call | solution.py:267
  47.1 0.0 collective-permute-done
  47.1 0.0 copy-done.1
  47.1 0.6 %add.3 = f32[24,73]{1,0:T(8,128)} add(f32[24,73]{1,0:T(8,128)S(1)} %copy-done.1, f32[24,73]{1,0:T(8,128)S(1)} %collective-permute-done) | non-fusion elementwise | flops 1752 | bytes 21024 | tf_op jit(solution)/shard_map/add | solution.py:263
Async XLA Ops:
  23.9 16.4 %all-to-all-start = ((bf16[16,48,128]{2,1,0:T(8,128)(2,1)}), bf16[16,48,128]{2,1,0:T(8,128)(2,1)S(1)}, u32[]{:S(2)}, u32[]{:S(2)}) async-start(bf16[16,48,128]{2,1,0:T(8,128)(2,1)} %spectral.1), calls=%async_computation | async-start | bytes 393216 | tf_op jit(solution)/shard_map/all_to_all | solution.py:244
  40.3 0.7 %copy-start = (bf16[16,48,128]{2,1,0:T(8,128)(2,1)}, bf16[16,48,128]{2,1,0:T(8,128)(2,1)S(1)}, u32[]{:S(2)}) copy-start(bf16[16,48,128]{2,1,0:T(8,128)(2,1)S(1)} %all-to-all-done.items_ref.refs_0_) | copy-start | bytes 589828
  42.6 4.5 %copy-start.1 = (f32[24,73]{1,0:T(8,128)S(1)}, f32[24,73]{1,0:T(8,128)}, u32[]{:S(2)}) copy-start(f32[24,73]{1,0:T(8,128)} %weight_rows.1) | copy-start | bytes 21028
  42.6 4.5 %collective-permute-start = (f32[24,73]{1,0:T(8,128)}, f32[24,73]{1,0:T(8,128)S(1)}, u32[]{:S(2)}, u32[]{:S(2)}) collective-permute-start(f32[24,73]{1,0:T(8,128)} %weight_rows.1), channel_id=1, source_target_pairs={{0,1},{1,0},{2,3},{3,2},{4,5},{5,4},{6,7},{7,6},{8,9},{9,8},{10,11... | collective-permute-start | bytes 21032 | tf_op jit(solution)/shard_map/ppermute | solution.py:263

commit v2 on v1

--- a/solution.py
+++ b/solution.py
@@ -9,6 +9,7 @@
 
 LON = 1440
 LANES = 128
+UNROLL = 4
 GROUP_AXES = ("order", "band")
 
 
@@ -37,7 +38,11 @@
     lats = legendre_hbm.shape[1]
     tiles = lane_tiles(degrees)
     saved_bufs = rest[: len(tiles)]
-    grad_wide, saved_wide, spec_wide, weight_acc, weight_turned, small_sem, grad_sem, saved_sem = rest[len(tiles):]
+    grad_wides = rest[len(tiles) : len(tiles) + UNROLL]
+    saved_wides = rest[len(tiles) + UNROLL : len(tiles) + 2 * UNROLL]
+    legendre_wide, tilted, spec_wide, weight_acc, weight_turned, small_sem, grad_sem, saved_sem = rest[len(tiles) + 2 * UNROLL :]
+    grad_pairs = grad_hbm.reshape(slots, 2 * degrees, embed)
+    saved_pairs = saved_hbm.reshape(slots, 2 * chan_in, degrees)
     small_copies = [
         pltpu.make_async_copy(source, target, small_sem.at[at])
         for at, (source, target) in enumerate([
@@ -47,13 +52,13 @@
     for copy in small_copies:
         copy.start()
     embed_tiles = embed // LANES
-    classes = slot_classes(slots, groups, degrees)
+    classes = slot_classes(slots, groups, degrees)[::-1]
 
     def grad_copies(slot, tile):
-        rows = pl.ds(tile * LANES, degrees - tile * LANES)
+        rows = pl.ds(2 * tile * LANES, 2 * (degrees - tile * LANES))
         return [
             pltpu.make_async_copy(
-                grad_hbm.at[slot, rows, :, pl.ds(at * LANES, LANES)],
+                grad_pairs.at[slot, rows, pl.ds(at * LANES, LANES)],
                 grad_buf.at[slot, at, rows],
                 grad_sem.at[slot, at],
             )
@@ -63,8 +68,8 @@
     def saved_copies(slot, tile):
         return [
             pltpu.make_async_copy(
-                saved_hbm.at[slot, :, :, pl.ds(*tiles[at])],
-                saved_bufs[at].at[slot, pl.ds(0, chan_in)],
+                saved_pairs.at[slot, :, pl.ds(*tiles[at])],
+                saved_bufs[at].at[slot, pl.ds(0, 2 * chan_in)],
                 saved_sem.at[slot, at],
             )
             for at in range(tile, len(tiles))
@@ -76,52 +81,73 @@
             for copy in grad_copies(slot, tile) + saved_copies(slot, tile):
                 copy.start()
 
-    spec_wide[...] = jnp.zeros_like(spec_wide)
     weight_acc[...] = jnp.zeros_like(weight_acc)
-    for at in range(embed_tiles):
-        grad_wide[at, 2 * degrees // 8 * 8 :] = jnp.zeros((grad_wide.shape[1] - 2 * degrees // 8 * 8, LANES), jnp.float32)
+    tilted[...] = jnp.zeros_like(tilted)
+    for wide in grad_wides:
+        for at in range(embed_tiles):
+            edge = 2 * degrees // 8 * 8
+            wide[at, edge:] = jnp.zeros((wide.shape[1] - edge, LANES), jnp.float32)
     for copy in small_copies:
         copy.wait()
     first_slot = (lax.axis_index("order") * lax.axis_size("band") + lax.axis_index("band")) * slots
     top = trunc_ref[0]
-    for tile, first, last in classes:
+
+    def run(slot_ids, tile):
         low = tile * LANES
         live = degrees - low
         live_pad = round_up(live, LANES)
-
-        @pl.loop(first, last)
-        def _(slot):
+        for slot in slot_ids:
             for copy in grad_copies(slot, tile) + saved_copies(slot, tile):
                 copy.wait()
+        total = None
+        for at_slot, slot in enumerate(slot_ids):
+            grad_wide, saved_wide = grad_wides[at_slot], saved_wides[at_slot]
             order = order_ref[first_slot + slot]
             degree = lax.broadcasted_iota(jnp.int32, (1, live_pad), 1) + low
             mask = (degree >= order) & (degree <= top)
             for at in range(embed_tiles):
-                pairs = grad_buf[slot, at, low:degrees].reshape(2 * live, LANES)
+                pairs = grad_buf[slot, at, 2 * low : 2 * degrees]
                 grad_wide[at, : 2 * live] = pairs.astype(jnp.float32)
             for at in range(tile, len(tiles)):
                 start, width = tiles[at]
-                pairs = saved_bufs[at][slot, :chan_in].reshape(2 * chan_in, width)
+                pairs = saved_bufs[at][slot, : 2 * chan_in]
                 saved_wide[at, : 2 * chan_in, :width] = pairs.astype(jnp.float32)
-            lat_rows = legendre_buf[slot, :, low:degrees]
-            lat_rows = jnp.where(mask[:, :live], lat_rows.astype(jnp.float32), 0.0).astype(jnp.bfloat16)
+                legendre_wide[at_slot, at, :, :width] = legendre_buf[slot, :, start : start + width].astype(jnp.float32)
             for part in range(2):
                 grads = jnp.concatenate(
                     [grad_wide[at, pl.ds(part, live_pad, stride=2)].astype(jnp.bfloat16) for at in range(embed_tiles)],
                     axis=1,
                 )
-                saved = jnp.concatenate(
-                    [saved_wide[at, pl.ds(part, chan_pad, stride=2)] for at in range(tile, len(tiles))], axis=1
+                left = jnp.concatenate(
+                    [
+                        jnp.concatenate(
+                            [legendre_wide[at_slot, at], saved_wide[at, pl.ds(part, chan_pad, stride=2)]], axis=0
+                        )
+                        for at in range(tile, len(tiles))
+                    ],
+                    axis=1,
                 )
-                saved = jnp.where(mask, saved, 0.0).astype(jnp.bfloat16)
-                lifted = lax.dot_general(
-                    grads, weight_buf[...], (((1,), (1,)), ((), ())), preferred_element_type=jnp.float32
-                ).astype(jnp.bfloat16)
-                spec = jnp.dot(lat_rows, lifted[:live], preferred_element_type=jnp.float32)
+                left = jnp.where(mask, left, 0.0).astype(jnp.bfloat16)
+                both = jnp.dot(left, grads, preferred_element_type=jnp.float32)
                 row = pl.multiple_of((part * pad_slots + slot) * lats, lats)
-                spec_wide[pl.ds(row, lats), :chan_in] = spec
-                weight_acc[:chan_pad] += jnp.dot(saved, grads, preferred_element_type=jnp.float32)
-
+                tilted[pl.ds(row, lats)] = both[:lats].astype(jnp.bfloat16)
+                total = both[lats:] if total is None else total + both[lats:]
+        weight_acc[:chan_pad] += total
+
+    for tile, first, last in classes:
+        count = len(grad_wides)
+        chunks = (last - first) // count
+
+        @pl.loop(0, chunks)
+        def _(chunk):
+            run([first + chunk * count + at for at in range(count)], tile)
+
+        if first + chunks * count < last:
+            run(list(range(first + chunks * count, last)), tile)
+
+    spec_wide[pl.ds(0, tilted.shape[0]), :chan_in] = lax.dot_general(
+        tilted[...], weight_buf[...], (((1,), (1,)), ((), ())), preferred_element_type=jnp.float32
+    )
     for at in range(embed_tiles):
         weight_turned[at * LANES : (at + 1) * LANES] = weight_acc[:, at * LANES : (at + 1) * LANES].T
     rows_dev = embed // groups
@@ -226,10 +252,12 @@
             pltpu.SMEM(trunc_degree.shape, jnp.int32),
             pltpu.VMEM((slots, lats, degrees), jnp.bfloat16),
             pltpu.VMEM((chan_in, embed), jnp.bfloat16),
-            pltpu.VMEM((slots, embed_tiles, round_up(degrees, 8), 2, LANES), jnp.bfloat16),
-            *[pltpu.VMEM((slots, round_up(chan_in, 8), 2, width), jnp.bfloat16) for _, width in tiles],
-            pltpu.VMEM((embed_tiles, 2 * round_up(degrees, LANES) + 8, LANES), jnp.float32),
-            pltpu.VMEM((len(tiles), 2 * round_up(chan_in, 8) + 8, LANES), jnp.float32),
+            pltpu.VMEM((slots, embed_tiles, round_up(2 * degrees, 16), LANES), jnp.bfloat16),
+            *[pltpu.VMEM((slots, round_up(2 * chan_in, 16), width), jnp.bfloat16) for _, width in tiles],
+            *[pltpu.VMEM((embed_tiles, 2 * round_up(degrees, LANES) + 8, LANES), jnp.float32)] * UNROLL,
+            *[pltpu.VMEM((len(tiles), 2 * round_up(chan_in, 8) + 8, LANES), jnp.float32)] * UNROLL,
+            pltpu.VMEM((UNROLL, len(tiles), lats, LANES), jnp.float32),
+            pltpu.VMEM((rows * lats, embed), jnp.bfloat16),
             pltpu.VMEM(((rows + 1) * lats, LANES), jnp.float32),
             pltpu.VMEM((LANES, embed), jnp.float32),
             pltpu.VMEM((embed, LANES), jnp.float32),

time: 48 us -> 32.6 us (0.68)
  Pallas kernels: 30.8 us -> 15.4 us
    pallas_call x1, Pallas kernels: 22.6 us -> 7.27 us  [local(): pl.pallas_call(lambda *refs: spectral_kernel(groups, pad_slots, *refs), o...]
  transfers between devices with their start and end apart: 2 -> 2, of which waited for: 1 -> 1; matrix products, arithmetic and copies ran while one was open for 0% -> 0% of each run, Pallas kernels for 14% -> 20%
where the time goes in v2:
time: 32.6 us; the launch traced here: 32.3 us
  Pallas kernels  15.4 us (47%)
  starting transfers between devices  8.88 us (27%)
  waiting for transfers between devices  5.42 us (17%)
  between operations  1.3 us (4%)
  local copies, waits for them, and re-layouts  0.69 us (2%)
  other arithmetic  0.6 us (2%)
    all_to_all x1, starting transfers between devices, local(): lax.all_to_all(packed, GROUP_AXES, split_axis=0, concat_axis=0, tiled=True)  7.36 us
    pallas_call x1, Pallas kernels, local(): pl.pallas_call(lambda *refs: spectral_kernel(groups, pad_slots, *refs), o...  7.27 us
    all_to_all x1, waiting for transfers between devices, local(): lax.all_to_all(packed, GROUP_AXES, split_axis=0, concat_axis=0, tiled=True)  5.42 us
    pallas_call x1, Pallas kernels, local(): pl.pallas_call(lambda *refs: table_kernel(groups, slots, *refs), out_shap...  3.58 us
    pallas_call x1, Pallas kernels, local(): pl.pallas_call(synthesis_kernel, out_shape=jax.ShapeDtypeStruct((chan_in,...  2.97 us
    pallas_call x1, Pallas kernels, local(): pl.pallas_call(lambda *refs: weight_kernel(chan_in, rows_dev, *refs), out...  1.62 us
    ppermute x1, starting transfers between devices, local(): weight_grad = own + lax.ppermute(own, 'chan', [(0, 1), (1, 0)])  1.52 us
    unnamed x4, local copies, waits for them, and re-layouts  0.69 us
  transfers between devices with their start and end apart: 2, of which 1 were waited for; matrix products, arithmetic and copies ran while one was open for 0% of the time, Pallas kernels for 20%

profile of v2, /device:TPU:0, one launch (start us, length us, event | category | flops | bytes accessed | tf_op | source)
XLA Modules:
  0.0 32.3 jit_solution(9437461672682443752)
XLA Ops:
  1.3 7.3 %spectral.1 = bf16[16,48,128]{2,1,0:T(8,128)(2,1)} custom-call(s32[368]{0:T(512)} %refs_0_.3, s32[1]{0:T(128)S(6)} %copy.8.refs_1_, bf16[23,361,2,384]{3,2,1,0:T(2,128)(2,1)} %bitcast.9, bf16[23,73,2,361]{3,2,1,0:T(2,128)(2,1)} %bitcast.10, bf16[23,16,361]{2,1,0:T(8,128)(2,1)} %bitcast.11, bf16[73,384]{1,0:T(8,128)(2,1)} %bitcast.13), custom_call_target="tpu_custom_call" | custom-call | tf_op jit(solution)/shard_map/spectral/pallas_call | solution.py:245
  8.6 7.4 %all-to-all-start = ((bf16[16,48,128]{2,1,0:T(8,128)(2,1)}), bf16[16,48,128]{2,1,0:T(8,128)(2,1)S(1)}, u32[]{:S(2)}, u32[]{:S(2)}) async-start(bf16[16,48,128]{2,1,0:T(8,128)(2,1)} %spectral.1), calls=%async_computation | async-start | bytes 393216 | tf_op jit(solution)/shard_map/all_to_all | solution.py:272
  15.9 3.6 %table.1.table_ref = bf16[768,1440]{1,0:T(8,128)(2,1)} custom-call(s32[368]{0:T(512)} %refs_0_.3), custom_call_target="tpu_custom_call" | custom-call | flops 20000000 | bytes 2211840 | tf_op jit(solution)/shard_map/table/pallas_call | solution.py:274
  19.5 5.4 %all-to-all-done.items_ref.refs_0_ = bf16[16,48,128]{2,1,0:T(8,128)(2,1)S(1)} async-done(((bf16[16,48,128]{2,1,0:T(8,128)(2,1)}), bf16[16,48,128]{2,1,0:T(8,128)(2,1)S(1)}, u32[]{:S(2)}, u32[]{:S(2)}) %all-to-all-start) | async-done | bytes 196640 | tf_op jit(solution)/shard_map/all_to_all | solution.py:272
  24.9 0.0 copy-start
  24.9 0.7 %copy-done = bf16[16,48,128]{2,1,0:T(8,128)(2,1)} copy-done((bf16[16,48,128]{2,1,0:T(8,128)(2,1)}, bf16[16,48,128]{2,1,0:T(8,128)(2,1)S(1)}, u32[]{:S(2)}) %copy-start) | copy-done | bytes 196632
  25.6 1.6 %weight_rows.1 = f32[24,73]{1,0:T(8,128)} custom-call(bf16[16,48,128]{2,1,0:T(8,128)(2,1)} %copy-done), custom_call_target="tpu_custom_call" | custom-call | tf_op jit(solution)/shard_map/weight_rows/pallas_call | solution.py:283
  27.2 0.0 copy-start.1
  27.2 1.5 %collective-permute-start = (f32[24,73]{1,0:T(8,128)}, f32[24,73]{1,0:T(8,128)S(1)}, u32[]{:S(2)}, u32[]{:S(2)}) collective-permute-start(f32[24,73]{1,0:T(8,128)} %weight_rows.1), channel_id=1, source_target_pairs={{0,1},{1,0},{2,3},{3,2},{4,5},{5,4},{6,7},{7,6},{8,9},{9,8},{10,11... | collective-permute-start | bytes 21032 | tf_op jit(solution)/shard_map/ppermute | solution.py:291
  28.7 3.0 %synthesis.1 = bf16[73,1440]{1,0:T(8,128)(2,1)} custom-call(bf16[16,48,128]{2,1,0:T(8,128)(2,1)} %copy-done, bf16[768,1440]{1,0:T(8,128)(2,1)} %table.1.table_ref), custom_call_target="tpu_custom_call" | custom-call | flops 283115520 | bytes 2211840 | tf_op jit(solution)/shard_map/synthesis/pallas_call | solution.py:295
  31.7 0.0 collective-permute-done
  31.7 0.0 copy-done.1
  31.7 0.6 %add.3 = f32[24,73]{1,0:T(8,128)} add(f32[24,73]{1,0:T(8,128)S(1)} %copy-done.1, f32[24,73]{1,0:T(8,128)S(1)} %collective-permute-done) | non-fusion elementwise | flops 1752 | bytes 21024 | tf_op jit(solution)/shard_map/add | solution.py:291
Async XLA Ops:
  8.6 16.4 %all-to-all-start = ((bf16[16,48,128]{2,1,0:T(8,128)(2,1)}), bf16[16,48,128]{2,1,0:T(8,128)(2,1)S(1)}, u32[]{:S(2)}, u32[]{:S(2)}) async-start(bf16[16,48,128]{2,1,0:T(8,128)(2,1)} %spectral.1), calls=%async_computation | async-start | bytes 393216 | tf_op jit(solution)/shard_map/all_to_all | solution.py:272
  24.9 0.7 %copy-start = (bf16[16,48,128]{2,1,0:T(8,128)(2,1)}, bf16[16,48,128]{2,1,0:T(8,128)(2,1)S(1)}, u32[]{:S(2)}) copy-start(bf16[16,48,128]{2,1,0:T(8,128)(2,1)S(1)} %all-to-all-done.items_ref.refs_0_) | copy-start | bytes 589828
  27.2 4.5 %copy-start.1 = (f32[24,73]{1,0:T(8,128)S(1)}, f32[24,73]{1,0:T(8,128)}, u32[]{:S(2)}) copy-start(f32[24,73]{1,0:T(8,128)} %weight_rows.1) | copy-start | bytes 21028
  27.2 4.5 %collective-permute-start = (f32[24,73]{1,0:T(8,128)}, f32[24,73]{1,0:T(8,128)S(1)}, u32[]{:S(2)}, u32[]{:S(2)}) collective-permute-start(f32[24,73]{1,0:T(8,128)} %weight_rows.1), channel_id=1, source_target_pairs={{0,1},{1,0},{2,3},{3,2},{4,5},{5,4},{6,7},{7,6},{8,9},{9,8},{10,11... | collective-permute-start | bytes 21032 | tf_op jit(solution)/shard_map/ppermute | solution.py:291

commit v3 on v2

--- a/solution.py
+++ b/solution.py
@@ -10,6 +10,7 @@
 LON = 1440
 LANES = 128
 UNROLL = 4
+SMALL_VMEM = 16 << 20
 GROUP_AXES = ("order", "band")
 
 
@@ -276,6 +277,7 @@
         out_shape=jax.ShapeDtypeStruct((groups * rows, LON), jnp.bfloat16),
         in_specs=[smem],
         out_specs=vmem,
+        compiler_params=pltpu.CompilerParams(vmem_limit_bytes=SMALL_VMEM),
         cost_estimate=pl.CostEstimate(flops=20_000_000, bytes_accessed=groups * rows * LON * 2, transcendentals=0),
         name="table",
     )(order_of_slot)
@@ -285,6 +287,7 @@
         out_shape=jax.ShapeDtypeStruct((rows_dev, chan_in), jnp.float32),
         in_specs=[vmem],
         out_specs=vmem,
+        compiler_params=pltpu.CompilerParams(vmem_limit_bytes=SMALL_VMEM),
         name="weight_rows",
     )(received)
     if samples == 2:
@@ -297,6 +300,7 @@
         out_shape=jax.ShapeDtypeStruct((chan_in, LON), jnp.bfloat16),
         in_specs=[vmem, vmem],
         out_specs=vmem,
+        compiler_params=pltpu.CompilerParams(vmem_limit_bytes=SMALL_VMEM),
         cost_estimate=pl.CostEstimate(flops=2 * groups * rows * LANES * LON, bytes_accessed=groups * rows * LON * 2, transcendentals=0),
         name="synthesis",
     )(received, table)

time: 32.6 us -> 29.6 us (0.908)
  Pallas kernels: 15.4 us -> 10.6 us
  waiting for transfers between devices: 5.42 us -> 7.95 us
  local copies, waits for them, and re-layouts: 0.69 us -> 0.01 us
    pallas_call x1, Pallas kernels: 2.97 us -> 1.18 us  [local(): pl.pallas_call(synthesis_kernel, out_shape=jax.ShapeDtypeStruct((chan_in,...]
    pallas_call x1, Pallas kernels: 3.58 us -> 2.03 us  [local(): pl.pallas_call(lambda *refs: table_kernel(groups, slots, *refs), out_shap...]
    all_to_all x1, waiting for transfers between devices: 5.42 us -> 6.95 us  [local(): lax.all_to_all(packed, GROUP_AXES, split_axis=0, concat_axis=0, tiled=True)]
    pallas_call x1, Pallas kernels: 1.62 us -> 0.09 us  [local(): pl.pallas_call(lambda *refs: weight_kernel(chan_in, rows_dev, *refs), out...]
    ppermute x1, waiting for transfers between devices: 0.01 us -> 1 us  [local(): weight_grad = own + lax.ppermute(own, 'chan', [(0, 1), (1, 0)])]
    unnamed x4 -> x2, local copies, waits for them, and re-layouts: 0.69 us -> 0.01 us
  transfers between devices with their start and end apart: 2 -> 2, of which waited for: 1 -> 2; matrix products, arithmetic and copies ran while one was open for 0% -> 0% of each run, Pallas kernels for 20% -> 11%
where the time goes in v3:
time: 29.6 us; the launch traced here: 29.3 us
  Pallas kernels  10.6 us (36%)
  starting transfers between devices  8.9 us (30%)
  waiting for transfers between devices  7.95 us (27%)
  between operations  1.32 us (4%)
  other arithmetic  0.6 us (2%)
    all_to_all x1, starting transfers between devices, local(): lax.all_to_all(packed, GROUP_AXES, split_axis=0, concat_axis=0, tiled=True)  7.37 us
    pallas_call x1, Pallas kernels, local(): pl.pallas_call(lambda *refs: spectral_kernel(groups, pad_slots, *refs), o...  7.27 us
    all_to_all x1, waiting for transfers between devices, local(): lax.all_to_all(packed, GROUP_AXES, split_axis=0, concat_axis=0, tiled=True)  6.95 us
    pallas_call x1, Pallas kernels, local(): pl.pallas_call(lambda *refs: table_kernel(groups, slots, *refs), out_shap...  2.03 us
    ppermute x1, starting transfers between devices, local(): weight_grad = own + lax.ppermute(own, 'chan', [(0, 1), (1, 0)])  1.53 us
    pallas_call x1, Pallas kernels, local(): pl.pallas_call(synthesis_kernel, out_shape=jax.ShapeDtypeStruct((chan_in,...  1.18 us
    ppermute x1, waiting for transfers between devices, local(): weight_grad = own + lax.ppermute(own, 'chan', [(0, 1), (1, 0)])  1 us
    add x1, other arithmetic, local(): weight_grad = own + lax.ppermute(own, 'chan', [(0, 1), (1, 0)])  0.6 us
  transfers between devices with their start and end apart: 2, of which 2 were waited for; matrix products, arithmetic and copies ran while one was open for 0% of the time, Pallas kernels for 11%

profile of v3, /device:TPU:0, one launch (start us, length us, event | category | flops | bytes accessed | tf_op | source)
XLA Modules:
  0.0 29.3 jit_solution(13894958694467400811)
XLA Ops:
  1.3 0.0 copy-start
  1.3 7.3 %spectral.1 = bf16[16,48,128]{2,1,0:T(8,128)(2,1)} custom-call(s32[368]{0:T(512)} %refs_0_.3, s32[1]{0:T(128)S(6)} %copy.8.refs_1_, bf16[23,361,2,384]{3,2,1,0:T(2,128)(2,1)} %bitcast.9, bf16[23,73,2,361]{3,2,1,0:T(2,128)(2,1)} %bitcast.10, bf16[23,16,361]{2,1,0:T(8,128)(2,1)} %bitcast.11, bf16[73,384]{1,0:T(8,128)(2,1)} %bitcast.13), custom_call_target="tpu_custom_call" | custom-call | tf_op jit(solution)/shard_map/spectral/pallas_call | solution.py:246
  8.6 7.4 %all-to-all-start = ((bf16[16,48,128]{2,1,0:T(8,128)(2,1)}), bf16[16,48,128]{2,1,0:T(8,128)(2,1)S(1)}, u32[]{:S(2)}, u32[]{:S(2)}) async-start(bf16[16,48,128]{2,1,0:T(8,128)(2,1)} %spectral.1), calls=%async_computation | async-start | bytes 393216 | tf_op jit(solution)/shard_map/all_to_all | solution.py:273
  15.9 0.0 copy-done
  16.0 2.0 %table.1.table_ref = bf16[768,1440]{1,0:T(8,128)(2,1)S(1)} custom-call(s32[368]{0:T(512)S(1)} %copy-done), custom_call_target="tpu_custom_call" | custom-call | flops 20000000 | bytes 2211840 | tf_op jit(solution)/shard_map/table/pallas_call | solution.py:275
  18.0 7.0 %all-to-all-done.items_ref.refs_0_ = bf16[16,48,128]{2,1,0:T(8,128)(2,1)S(1)} async-done(((bf16[16,48,128]{2,1,0:T(8,128)(2,1)}), bf16[16,48,128]{2,1,0:T(8,128)(2,1)S(1)}, u32[]{:S(2)}, u32[]{:S(2)}) %all-to-all-start) | async-done | bytes 196640 | tf_op jit(solution)/shard_map/all_to_all | solution.py:273
  24.9 0.1 weight_rows.1
  25.0 1.5 %collective-permute-start = (f32[24,73]{1,0:T(8,128)S(1)}, f32[24,73]{1,0:T(8,128)S(1)}, u32[]{:S(2)}, u32[]{:S(2)}) collective-permute-start(f32[24,73]{1,0:T(8,128)S(1)} %weight_rows.1), channel_id=1, source_target_pairs={{0,1},{1,0},{2,3},{3,2},{4,5},{5,4},{6,7},{7,6},{8,9},{9,8},{10,11... | collective-permute-start | bytes 21032 | tf_op jit(solution)/shard_map/ppermute | solution.py:294
  26.6 1.2 %synthesis.1 = bf16[73,1440]{1,0:T(8,128)(2,1)} custom-call(bf16[16,48,128]{2,1,0:T(8,128)(2,1)S(1)} %all-to-all-done.items_ref.refs_0_, bf16[768,1440]{1,0:T(8,128)(2,1)S(1)} %table.1.table_ref), custom_call_target="tpu_custom_call" | custom-call | flops 283115520 | bytes 2211840 | tf_op jit(solution)/shard_map/synthesis/pallas_call | solution.py:298
  27.7 1.0 %collective-permute-done = f32[24,73]{1,0:T(8,128)S(1)} collective-permute-done((f32[24,73]{1,0:T(8,128)S(1)}, f32[24,73]{1,0:T(8,128)S(1)}, u32[]{:S(2)}, u32[]{:S(2)}) %collective-permute-start) | collective-permute-done | bytes 7040 | tf_op jit(solution)/shard_map/ppermute | solution.py:294
  28.7 0.6 %add.3 = f32[24,73]{1,0:T(8,128)} add(f32[24,73]{1,0:T(8,128)S(1)} %weight_rows.1, f32[24,73]{1,0:T(8,128)S(1)} %collective-permute-done) | non-fusion elementwise | flops 1752 | bytes 21024 | tf_op jit(solution)/shard_map/add | solution.py:294
Async XLA Ops:
  1.3 14.7 %copy-start = (s32[368]{0:T(512)S(1)}, s32[368]{0:T(512)}, u32[]{:S(2)}) copy-start(s32[368]{0:T(512)} %refs_0_.3) | copy-start | bytes 4420
  8.6 16.4 %all-to-all-start = ((bf16[16,48,128]{2,1,0:T(8,128)(2,1)}), bf16[16,48,128]{2,1,0:T(8,128)(2,1)S(1)}, u32[]{:S(2)}, u32[]{:S(2)}) async-start(bf16[16,48,128]{2,1,0:T(8,128)(2,1)} %spectral.1), calls=%async_computation | async-start | bytes 393216 | tf_op jit(solution)/shard_map/all_to_all | solution.py:273
  25.0 3.7 %collective-permute-start = (f32[24,73]{1,0:T(8,128)S(1)}, f32[24,73]{1,0:T(8,128)S(1)}, u32[]{:S(2)}, u32[]{:S(2)}) collective-permute-start(f32[24,73]{1,0:T(8,128)S(1)} %weight_rows.1), channel_id=1, source_target_pairs={{0,1},{1,0},{2,3},{3,2},{4,5},{5,4},{6,7},{7,6},{8,9},{9,8},{10,11... | collective-permute-start | bytes 21032 | tf_op jit(solution)/shard_map/ppermute | solution.py:294

commit v4 on v3

--- a/solution.py
+++ b/solution.py
@@ -55,32 +55,38 @@
     embed_tiles = embed // LANES
     classes = slot_classes(slots, groups, degrees)[::-1]
 
-    def grad_copies(slot, tile):
+    def copies(slot, tile, turn):
         rows = pl.ds(2 * tile * LANES, 2 * (degrees - tile * LANES))
         return [
             pltpu.make_async_copy(
-                grad_pairs.at[slot, rows, pl.ds(at * LANES, LANES)],
-                grad_buf.at[slot, at, rows],
-                grad_sem.at[slot, at],
+                grad_pairs.at[slot, rows, pl.ds(at * LANES, LANES)], grad_buf.at[slot, at, rows], grad_sem.at[turn]
             )
             for at in range(embed_tiles)
-        ]
-
-    def saved_copies(slot, tile):
-        return [
+        ] + [
             pltpu.make_async_copy(
                 saved_pairs.at[slot, :, pl.ds(*tiles[at])],
                 saved_bufs[at].at[slot, pl.ds(0, 2 * chan_in)],
-                saved_sem.at[slot, at],
+                saved_sem.at[turn, at],
             )
             for at in range(tile, len(tiles))
         ]
 
+    def arrivals(first, count, tile, turn):
+        span = pl.ds(first, count)
+        rows = pl.ds(2 * tile * LANES, 2 * (degrees - tile * LANES))
+        landed = [(grad_buf.at[span, :, rows], grad_sem.at[turn])] + [
+            (saved_bufs[at].at[span, pl.ds(0, 2 * chan_in)], saved_sem.at[turn, at]) for at in range(tile, len(tiles))
+        ]
+        return [pltpu.make_async_copy(place, place, sem) for place, sem in landed]
+
+    turn_of = 0
     for tile, first, last in classes:
         @pl.loop(first, last)
         def _(slot):
-            for copy in grad_copies(slot, tile) + saved_copies(slot, tile):
+            for copy in copies(slot, tile, turn_of + lax.div(slot - first, UNROLL)):
                 copy.start()
+
+        turn_of += -(-(last - first) // UNROLL)
 
     weight_acc[...] = jnp.zeros_like(weight_acc)
     tilted[...] = jnp.zeros_like(tilted)
@@ -93,13 +99,13 @@
     first_slot = (lax.axis_index("order") * lax.axis_size("band") + lax.axis_index("band")) * slots
     top = trunc_ref[0]
 
-    def run(slot_ids, tile):
+    def run(first_slot_id, count, tile, turn):
+        slot_ids = [first_slot_id + at for at in range(count)]
         low = tile * LANES
         live = degrees - low
         live_pad = round_up(live, LANES)
-        for slot in slot_ids:
-            for copy in grad_copies(slot, tile) + saved_copies(slot, tile):
-                copy.wait()
+        for copy in arrivals(first_slot_id, count, tile, turn):
+            copy.wait()
         total = None
         for at_slot, slot in enumerate(slot_ids):
             grad_wide, saved_wide = grad_wides[at_slot], saved_wides[at_slot]
@@ -135,16 +141,18 @@
                 total = both[lats:] if total is None else total + both[lats:]
         weight_acc[:chan_pad] += total
 
+    turn_of = 0
     for tile, first, last in classes:
-        count = len(grad_wides)
-        chunks = (last - first) // count
+        chunks = (last - first) // UNROLL
 
         @pl.loop(0, chunks)
         def _(chunk):
-            run([first + chunk * count + at for at in range(count)], tile)
-
-        if first + chunks * count < last:
-            run(list(range(first + chunks * count, last)), tile)
+            run(first + chunk * UNROLL, UNROLL, tile, turn_of + chunk)
+
+        turn_of += chunks
+        if first + chunks * UNROLL < last:
+            run(first + chunks * UNROLL, last - first - chunks * UNROLL, tile, turn_of)
+            turn_of += 1
 
     spec_wide[pl.ds(0, tilted.shape[0]), :chan_in] = lax.dot_general(
         tilted[...], weight_buf[...], (((1,), (1,)), ((), ())), preferred_element_type=jnp.float32
@@ -236,6 +244,7 @@
     rows = 2 * pad_slots
     embed_tiles = embed // LANES
     tiles = lane_tiles(degrees)
+    turns = sum(-(-(last - first) // UNROLL) for _, first, last in slot_classes(slots, groups, degrees))
     assert coef_grad.shape[0] == 1 and lats == groups and 2 * (LANES - chan_in) >= chan_in
 
     smem = pl.BlockSpec(memory_space=pltpu.SMEM)
@@ -263,8 +272,8 @@
             pltpu.VMEM((LANES, embed), jnp.float32),
             pltpu.VMEM((embed, LANES), jnp.float32),
             pltpu.SemaphoreType.DMA((4,)),
-            pltpu.SemaphoreType.DMA((slots, embed_tiles)),
-            pltpu.SemaphoreType.DMA((slots, len(tiles))),
+            pltpu.SemaphoreType.DMA((turns,)),
+            pltpu.SemaphoreType.DMA((turns, len(tiles))),
         ],
         compiler_params=pltpu.CompilerParams(vmem_limit_bytes=60 << 20),
         name="spectral",

time: 29.6 us -> 28.6 us (0.966)
  Pallas kernels: 10.6 us -> 9.52 us
    pallas_call x1, Pallas kernels: 7.27 us -> 6.22 us  [local(): pl.pallas_call(lambda *refs: spectral_kernel(groups, pad_slots, *refs), o...]
where the time goes in v4:
time: 28.6 us; the launch traced here: 28.3 us
  Pallas kernels  9.52 us (33%)
  starting transfers between devices  8.89 us (31%)
  waiting for transfers between devices  7.94 us (28%)
  between operations  1.32 us (5%)
  other arithmetic  0.6 us (2%)
    all_to_all x1, starting transfers between devices, local(): lax.all_to_all(packed, GROUP_AXES, split_axis=0, concat_axis=0, tiled=True)  7.36 us
    all_to_all x1, waiting for transfers between devices, local(): lax.all_to_all(packed, GROUP_AXES, split_axis=0, concat_axis=0, tiled=True)  6.95 us
    pallas_call x1, Pallas kernels, local(): pl.pallas_call(lambda *refs: spectral_kernel(groups, pad_slots, *refs), o...  6.22 us
    pallas_call x1, Pallas kernels, local(): pl.pallas_call(lambda *refs: table_kernel(groups, slots, *refs), out_shap...  2.03 us
    ppermute x1, starting transfers between devices, local(): weight_grad = own + lax.ppermute(own, 'chan', [(0, 1), (1, 0)])  1.54 us
    pallas_call x1, Pallas kernels, local(): pl.pallas_call(synthesis_kernel, out_shape=jax.ShapeDtypeStruct((chan_in,...  1.18 us
    ppermute x1, waiting for transfers between devices, local(): weight_grad = own + lax.ppermute(own, 'chan', [(0, 1), (1, 0)])  0.99 us
    add x1, other arithmetic, local(): weight_grad = own + lax.ppermute(own, 'chan', [(0, 1), (1, 0)])  0.6 us
  transfers between devices with their start and end apart: 2, of which 2 were waited for; matrix products, arithmetic and copies ran while one was open for 0% of the time, Pallas kernels for 11%

profile of v4, /device:TPU:0, one launch (start us, length us, event | category | flops | bytes accessed | tf_op | source)
XLA Modules:
  0.0 28.3 jit_solution(11280066986968407710)
XLA Ops:
  1.3 0.0 copy-start
  1.3 6.2 %spectral.1 = bf16[16,48,128]{2,1,0:T(8,128)(2,1)} custom-call(s32[368]{0:T(512)} %refs_0_.3, s32[1]{0:T(128)S(6)} %copy.8.refs_1_, bf16[23,361,2,384]{3,2,1,0:T(2,128)(2,1)} %bitcast.9, bf16[23,73,2,361]{3,2,1,0:T(2,128)(2,1)} %bitcast.10, bf16[23,16,361]{2,1,0:T(8,128)(2,1)} %bitcast.11, bf16[73,384]{1,0:T(8,128)(2,1)} %bitcast.13), custom_call_target="tpu_custom_call" | custom-call | tf_op jit(solution)/shard_map/spectral/pallas_call | solution.py:255
  7.5 7.4 %all-to-all-start = ((bf16[16,48,128]{2,1,0:T(8,128)(2,1)}), bf16[16,48,128]{2,1,0:T(8,128)(2,1)S(1)}, u32[]{:S(2)}, u32[]{:S(2)}) async-start(bf16[16,48,128]{2,1,0:T(8,128)(2,1)} %spectral.1), calls=%async_computation | async-start | bytes 393216 | tf_op jit(solution)/shard_map/all_to_all | solution.py:282
  14.9 0.0 copy-done
  14.9 2.0 %table.1.table_ref = bf16[768,1440]{1,0:T(8,128)(2,1)S(1)} custom-call(s32[368]{0:T(512)S(1)} %copy-done), custom_call_target="tpu_custom_call" | custom-call | flops 20000000 | bytes 2211840 | tf_op jit(solution)/shard_map/table/pallas_call | solution.py:284
  16.9 7.0 %all-to-all-done.items_ref.refs_0_ = bf16[16,48,128]{2,1,0:T(8,128)(2,1)S(1)} async-done(((bf16[16,48,128]{2,1,0:T(8,128)(2,1)}), bf16[16,48,128]{2,1,0:T(8,128)(2,1)S(1)}, u32[]{:S(2)}, u32[]{:S(2)}) %all-to-all-start) | async-done | bytes 196640 | tf_op jit(solution)/shard_map/all_to_all | solution.py:282
  23.9 0.1 weight_rows.1
  24.0 1.5 %collective-permute-start = (f32[24,73]{1,0:T(8,128)S(1)}, f32[24,73]{1,0:T(8,128)S(1)}, u32[]{:S(2)}, u32[]{:S(2)}) collective-permute-start(f32[24,73]{1,0:T(8,128)S(1)} %weight_rows.1), channel_id=1, source_target_pairs={{0,1},{1,0},{2,3},{3,2},{4,5},{5,4},{6,7},{7,6},{8,9},{9,8},{10,11... | collective-permute-start | bytes 21032 | tf_op jit(solution)/shard_map/ppermute | solution.py:303
  25.5 1.2 %synthesis.1 = bf16[73,1440]{1,0:T(8,128)(2,1)} custom-call(bf16[16,48,128]{2,1,0:T(8,128)(2,1)S(1)} %all-to-all-done.items_ref.refs_0_, bf16[768,1440]{1,0:T(8,128)(2,1)S(1)} %table.1.table_ref), custom_call_target="tpu_custom_call" | custom-call | flops 283115520 | bytes 2211840 | tf_op jit(solution)/shard_map/synthesis/pallas_call | solution.py:307
  26.7 1.0 %collective-permute-done = f32[24,73]{1,0:T(8,128)S(1)} collective-permute-done((f32[24,73]{1,0:T(8,128)S(1)}, f32[24,73]{1,0:T(8,128)S(1)}, u32[]{:S(2)}, u32[]{:S(2)}) %collective-permute-start) | collective-permute-done | bytes 7040 | tf_op jit(solution)/shard_map/ppermute | solution.py:303
  27.7 0.6 %add.3 = f32[24,73]{1,0:T(8,128)} add(f32[24,73]{1,0:T(8,128)S(1)} %weight_rows.1, f32[24,73]{1,0:T(8,128)S(1)} %collective-permute-done) | non-fusion elementwise | flops 1752 | bytes 21024 | tf_op jit(solution)/shard_map/add | solution.py:303
Async XLA Ops:
  1.3 13.6 %copy-start = (s32[368]{0:T(512)S(1)}, s32[368]{0:T(512)}, u32[]{:S(2)}) copy-start(s32[368]{0:T(512)} %refs_0_.3) | copy-start | bytes 4420
  7.5 16.4 %all-to-all-start = ((bf16[16,48,128]{2,1,0:T(8,128)(2,1)}), bf16[16,48,128]{2,1,0:T(8,128)(2,1)S(1)}, u32[]{:S(2)}, u32[]{:S(2)}) async-start(bf16[16,48,128]{2,1,0:T(8,128)(2,1)} %spectral.1), calls=%async_computation | async-start | bytes 393216 | tf_op jit(solution)/shard_map/all_to_all | solution.py:282
  24.0 3.7 %collective-permute-start = (f32[24,73]{1,0:T(8,128)S(1)}, f32[24,73]{1,0:T(8,128)S(1)}, u32[]{:S(2)}, u32[]{:S(2)}) collective-permute-start(f32[24,73]{1,0:T(8,128)S(1)} %weight_rows.1), channel_id=1, source_target_pairs={{0,1},{1,0},{2,3},{3,2},{4,5},{5,4},{6,7},{7,6},{8,9},{9,8},{10,11... | collective-permute-start | bytes 21032 | tf_op jit(solution)/shard_map/ppermute | solution.py:303

commit v5 on v4

--- a/solution.py
+++ b/solution.py
@@ -89,7 +89,11 @@
         turn_of += -(-(last - first) // UNROLL)
 
     weight_acc[...] = jnp.zeros_like(weight_acc)
-    tilted[...] = jnp.zeros_like(tilted)
+    filled = max(last for _, _, last in classes)
+    for part in range(2):
+        start, stop = (part * pad_slots + filled) * lats, (part + 1) * pad_slots * lats
+        if start < stop:
+            tilted[start:stop] = jnp.zeros((stop - start, embed), jnp.bfloat16)
     for wide in grad_wides:
         for at in range(embed_tiles):
             edge = 2 * degrees // 8 * 8

time: 28.6 us -> 28.6 us (level)
  no operation moved by 1% of the time
where the time goes in v5:
time: 28.6 us; the launch traced here: 28.3 us
  Pallas kernels  9.52 us (33%)
  starting transfers between devices  8.89 us (31%)
  waiting for transfers between devices  7.94 us (28%)
  between operations  1.32 us (5%)
  other arithmetic  0.6 us (2%)
    all_to_all x1, starting transfers between devices, local(): lax.all_to_all(packed, GROUP_AXES, split_axis=0, concat_axis=0, tiled=True)  7.36 us
    all_to_all x1, waiting for transfers between devices, local(): lax.all_to_all(packed, GROUP_AXES, split_axis=0, concat_axis=0, tiled=True)  6.95 us
    pallas_call x1, Pallas kernels, local(): pl.pallas_call(lambda *refs: spectral_kernel(groups, pad_slots, *refs), o...  6.22 us
    pallas_call x1, Pallas kernels, local(): pl.pallas_call(lambda *refs: table_kernel(groups, slots, *refs), out_shap...  2.03 us
    ppermute x1, starting transfers between devices, local(): weight_grad = own + lax.ppermute(own, 'chan', [(0, 1), (1, 0)])  1.54 us
    pallas_call x1, Pallas kernels, local(): pl.pallas_call(synthesis_kernel, out_shape=jax.ShapeDtypeStruct((chan_in,...  1.18 us
    ppermute x1, waiting for transfers between devices, local(): weight_grad = own + lax.ppermute(own, 'chan', [(0, 1), (1, 0)])  0.99 us
    add x1, other arithmetic, local(): weight_grad = own + lax.ppermute(own, 'chan', [(0, 1), (1, 0)])  0.6 us
  transfers between devices with their start and end apart: 2, of which 2 were waited for; matrix products, arithmetic and copies ran while one was open for 0% of the time, Pallas kernels for 11%

profile of v5, /device:TPU:0, one launch (start us, length us, event | category | flops | bytes accessed | tf_op | source)
XLA Modules:
  0.0 28.3 jit_solution(14689816821469781255)
XLA Ops:
  1.3 0.0 copy-start
  1.3 6.2 %spectral.1 = bf16[16,48,128]{2,1,0:T(8,128)(2,1)} custom-call(s32[368]{0:T(512)} %refs_0_.3, s32[1]{0:T(128)S(6)} %copy.8.refs_1_, bf16[23,361,2,384]{3,2,1,0:T(2,128)(2,1)} %bitcast.9, bf16[23,73,2,361]{3,2,1,0:T(2,128)(2,1)} %bitcast.10, bf16[23,16,361]{2,1,0:T(8,128)(2,1)} %bitcast.11, bf16[73,384]{1,0:T(8,128)(2,1)} %bitcast.13), custom_call_target="tpu_custom_call" | custom-call | tf_op jit(solution)/shard_map/spectral/pallas_call | solution.py:259
  7.5 7.4 %all-to-all-start = ((bf16[16,48,128]{2,1,0:T(8,128)(2,1)}), bf16[16,48,128]{2,1,0:T(8,128)(2,1)S(1)}, u32[]{:S(2)}, u32[]{:S(2)}) async-start(bf16[16,48,128]{2,1,0:T(8,128)(2,1)} %spectral.1), calls=%async_computation | async-start | bytes 393216 | tf_op jit(solution)/shard_map/all_to_all | solution.py:286
  14.9 0.0 copy-done
  14.9 2.0 %table.1.table_ref = bf16[768,1440]{1,0:T(8,128)(2,1)S(1)} custom-call(s32[368]{0:T(512)S(1)} %copy-done), custom_call_target="tpu_custom_call" | custom-call | flops 20000000 | bytes 2211840 | tf_op jit(solution)/shard_map/table/pallas_call | solution.py:288
  16.9 7.0 %all-to-all-done.items_ref.refs_0_ = bf16[16,48,128]{2,1,0:T(8,128)(2,1)S(1)} async-done(((bf16[16,48,128]{2,1,0:T(8,128)(2,1)}), bf16[16,48,128]{2,1,0:T(8,128)(2,1)S(1)}, u32[]{:S(2)}, u32[]{:S(2)}) %all-to-all-start) | async-done | bytes 196640 | tf_op jit(solution)/shard_map/all_to_all | solution.py:286
  23.9 0.1 weight_rows.1
  24.0 1.5 %collective-permute-start = (f32[24,73]{1,0:T(8,128)S(1)}, f32[24,73]{1,0:T(8,128)S(1)}, u32[]{:S(2)}, u32[]{:S(2)}) collective-permute-start(f32[24,73]{1,0:T(8,128)S(1)} %weight_rows.1), channel_id=1, source_target_pairs={{0,1},{1,0},{2,3},{3,2},{4,5},{5,4},{6,7},{7,6},{8,9},{9,8},{10,11... | collective-permute-start | bytes 21032 | tf_op jit(solution)/shard_map/ppermute | solution.py:307
  25.5 1.2 %synthesis.1 = bf16[73,1440]{1,0:T(8,128)(2,1)} custom-call(bf16[16,48,128]{2,1,0:T(8,128)(2,1)S(1)} %all-to-all-done.items_ref.refs_0_, bf16[768,1440]{1,0:T(8,128)(2,1)S(1)} %table.1.table_ref), custom_call_target="tpu_custom_call" | custom-call | flops 283115520 | bytes 2211840 | tf_op jit(solution)/shard_map/synthesis/pallas_call | solution.py:311
  26.7 1.0 %collective-permute-done = f32[24,73]{1,0:T(8,128)S(1)} collective-permute-done((f32[24,73]{1,0:T(8,128)S(1)}, f32[24,73]{1,0:T(8,128)S(1)}, u32[]{:S(2)}, u32[]{:S(2)}) %collective-permute-start) | collective-permute-done | bytes 7040 | tf_op jit(solution)/shard_map/ppermute | solution.py:307
  27.7 0.6 %add.3 = f32[24,73]{1,0:T(8,128)} add(f32[24,73]{1,0:T(8,128)S(1)} %weight_rows.1, f32[24,73]{1,0:T(8,128)S(1)} %collective-permute-done) | non-fusion elementwise | flops 1752 | bytes 21024 | tf_op jit(solution)/shard_map/add | solution.py:307
Async XLA Ops:
  1.3 13.6 %copy-start = (s32[368]{0:T(512)S(1)}, s32[368]{0:T(512)}, u32[]{:S(2)}) copy-start(s32[368]{0:T(512)} %refs_0_.3) | copy-start | bytes 4420
  7.5 16.4 %all-to-all-start = ((bf16[16,48,128]{2,1,0:T(8,128)(2,1)}), bf16[16,48,128]{2,1,0:T(8,128)(2,1)S(1)}, u32[]{:S(2)}, u32[]{:S(2)}) async-start(bf16[16,48,128]{2,1,0:T(8,128)(2,1)} %spectral.1), calls=%async_computation | async-start | bytes 393216 | tf_op jit(solution)/shard_map/all_to_all | solution.py:286
  24.0 3.7 %collective-permute-start = (f32[24,73]{1,0:T(8,128)S(1)}, f32[24,73]{1,0:T(8,128)S(1)}, u32[]{:S(2)}, u32[]{:S(2)}) collective-permute-start(f32[24,73]{1,0:T(8,128)S(1)} %weight_rows.1), channel_id=1, source_target_pairs={{0,1},{1,0},{2,3},{3,2},{4,5},{5,4},{6,7},{7,6},{8,9},{9,8},{10,11... | collective-permute-start | bytes 21032 | tf_op jit(solution)/shard_map/ppermute | solution.py:307
